TPU v7x, 32 devices: a whole 2x2x4 slice. The times are simulated.
32 devices in a mesh: dp: 4 (over z), pipe: 4 (over x, core), ctx: 2 (over y).
Axes of the slice: x: 2, y: 2, z: 4, core: 2. Of those that a mesh axis runs over, the one named last changes fastest.
Arguments:
- projected: bfloat16 [4, 4, 256, 2304], P('pipe', 'dp', 'ctx'), may hold values from -40 to 40
- gated_input: bfloat16 [4, 4, 256, 1536], P('pipe', 'dp', 'ctx'), may hold values from -6 to 6
- upstream: bfloat16 [4, 4, 256, 2304], P('pipe', 'dp', 'ctx'), may hold values from -6 to 6
- lengths: int32 [4, 4], P('pipe', 'dp'), may hold values from 64 to 256, as said below
- depth_kernel: float32 [4, 31, 1536], P('pipe'), may hold values from -1 to 1
- depth_bias: float32 [4, 1536], P('pipe'), may hold values from -3 to 3
Outputs:
- attention_out: bfloat16 [4, 4, 256, 768], P('pipe', 'dp', 'ctx')
- depth_out: bfloat16 [4, 4, 256, 1536], P('pipe', 'dp', 'ctx')
- projected_grad: bfloat16 [4, 4, 256, 2304], P('pipe', 'dp', 'ctx')
- gated_grad: bfloat16 [4, 4, 256, 1536], P('pipe', 'dp', 'ctx')
- kernel_grad: float32 [4, 31, 1536], P('pipe')
- bias_grad: float32 [4, 1536], P('pipe')
Inputs may be any that keep to these rules, and one draw needn't show every extreme that they name: `lengths`: frames after a recording's length are padding; in every draw some recording has all 256 frames.
All inputs are finite; a program needn't handle non-finite values.
Results may differ from a plain program's by a relative error of at most 0.0069.
Values may be sent and summed in bfloat16 or wider, within the bound.
No kernel may reach another device: no remote copies, remote signals or barrier semaphores. Data moves between devices by JAX's collectives and lax.ppermute only.
A program may use at most 64 MiB of HBM per device.

v0:
```python
import math
import jax
import jax.numpy as jnp
from jax import lax
from jax.sharding import PartitionSpec as P

HEADS = 8
HD = 96
KSIZE = 31


def shifted(value, axis, by):
    count = lax.axis_size(axis)
    return lax.ppermute(value, axis, [(i, (i + by) % count) for i in range(count)])


def padded_2(block, sides, width):
    for axis, dim in sides:
        count = lax.axis_size(axis)
        forward = [(i, i + 1) for i in range(count - 1)]
        backward = [(target, source) for source, target in forward]
        low = lax.ppermute(
            lax.slice_in_dim(block, block.shape[dim] - width, None, axis=dim), axis, forward
        )
        high = lax.ppermute(lax.slice_in_dim(block, 0, width, axis=dim), axis, backward)
        block = jnp.concatenate([low, block, high], axis=dim)
    return block


def head_pass(queries, grad_out, keys_in, values_in, valid_keys):
    query_rows, head_dim = queries.shape
    score_scale = 1.0 / math.sqrt(head_dim)
    block_rows = min(512, query_rows)
    block_count = query_rows // block_rows
    frame_count = keys_in.shape[0]
    across = (((1,), (1,)), ((), ()))
    downward = (((0,), (0,)), ((), ()))

    def advance(totals, blocks):
        query_block, grad_block = blocks
        scores = (
            lax.dot_general(query_block, keys_in, across, preferred_element_type=jnp.float32)
            * score_scale
        )
        scores = jnp.where(valid_keys[None, :], scores, -1e30)
        row_top = jnp.max(scores, axis=1, keepdims=True)
        row_total = jnp.sum(jnp.exp(scores - row_top), axis=1, keepdims=True)
        probs_bf = (jnp.exp(scores - row_top) / row_total).astype(jnp.bfloat16)
        attended_full = jnp.dot(probs_bf, values_in, preferred_element_type=jnp.float32)
        attended = attended_full.astype(jnp.bfloat16)
        grad_probs = lax.dot_general(
            grad_block, values_in, across, preferred_element_type=jnp.float32
        )
        centre = jnp.sum(grad_block.astype(jnp.float32) * attended_full, axis=1, keepdims=True)
        grad_scores = (probs_bf.astype(jnp.float32) * (grad_probs - centre) * score_scale).astype(
            jnp.bfloat16
        )
        grad_query = jnp.dot(grad_scores, keys_in, preferred_element_type=jnp.float32).astype(
            jnp.bfloat16
        )
        key_total = totals[0] + lax.dot_general(
            grad_scores, query_block, downward, preferred_element_type=jnp.float32
        )
        value_total = totals[1] + lax.dot_general(
            probs_bf, grad_block, downward, preferred_element_type=jnp.float32
        )
        return ((key_total, value_total), (attended, grad_query))

    zero_grads = jnp.zeros((frame_count, head_dim), jnp.float32)
    blocked = (
        queries.reshape(block_count, block_rows, head_dim),
        grad_out.reshape(block_count, block_rows, head_dim),
    )
    totals, results = lax.scan(advance, (zero_grads, zero_grads), blocked)
    attended = results[0].reshape(query_rows, head_dim)
    grad_query = results[1].reshape(query_rows, head_dim)
    return (attended, grad_query, totals[0], totals[1])


def attend_block(query_part, grad_part, key_value, valid_keys, heads_dev):
    block_width = heads_dev * HD

    def split_heads(matrix):
        return matrix.reshape(matrix.shape[0], heads_dev, HD).transpose(1, 0, 2)

    def join_heads(matrix):
        return matrix.transpose(1, 0, 2).reshape(matrix.shape[1], block_width)

    def one_head(items):
        return head_pass(items[0], items[1], items[2], items[3], valid_keys)

    stacked = (
        split_heads(query_part),
        split_heads(grad_part),
        split_heads(key_value[:, :block_width]),
        split_heads(key_value[:, block_width:]),
    )
    attended, grad_query, key_grad, value_grad = lax.map(one_head, stacked)
    key_grads = jnp.concatenate([join_heads(key_grad), join_heads(value_grad)], axis=1)
    return (join_heads(attended), join_heads(grad_query), key_grads)


def depthwise(source, taps, bias, count):
    total = jnp.zeros((count, source.shape[1]), jnp.float32) + bias[None, :]
    for offset in range(KSIZE):
        total = total + taps[offset][None, :] * source[offset : offset + count].astype(jnp.float32)
    return total


def slope(pre_act):
    sigmoid_pre = jax.nn.sigmoid(pre_act)
    return sigmoid_pre + pre_act * sigmoid_pre * (1.0 - sigmoid_pre)


def local(projected, gated_input, upstream, lengths, depth_kernel, depth_bias):
    arriving = shifted(upstream, "pipe", -1)[0, 0]
    rows_here = projected.shape[2]
    devices_ctx = lax.axis_size("ctx")
    frames_all = rows_here * devices_ctx
    embed = HEADS * HD
    part_count = max(devices_ctx // HEADS, 1)
    heads_dev = max(HEADS // devices_ctx, 1)
    block_heads = HEADS // heads_dev
    part_rows = rows_here // part_count
    block_width = heads_dev * HD
    my_index = lax.axis_index("ctx")
    length = lengths[0, 0]
    valid_keys = jnp.arange(frames_all) < length
    frame_mask = my_index * rows_here + jnp.arange(rows_here) < length
    mixed = projected[0, 0]
    queries = mixed[:, :embed]
    keys_in = mixed[:, embed : 2 * embed]
    values_in = mixed[:, 2 * embed :]
    grad_attn = arriving[:, :embed]
    grad_depth = arriving[:, embed:]

    def by_part(matrix):
        split = matrix.reshape(part_count, part_rows, block_heads, block_width).transpose(
            2, 0, 1, 3
        )
        return split.reshape(devices_ctx, part_rows, block_width)

    key_value = jnp.concatenate(
        [
            keys_in.reshape(rows_here, block_heads, block_width),
            values_in.reshape(rows_here, block_heads, block_width),
        ],
        axis=2,
    )
    key_value = jnp.repeat(key_value.transpose(1, 0, 2), part_count, axis=0)
    query_part, grad_part, key_value = (
        lax.all_to_all(by_part(queries), "ctx", split_axis=0, concat_axis=1, tiled=True),
        lax.all_to_all(by_part(grad_attn), "ctx", split_axis=0, concat_axis=1, tiled=True),
        lax.all_to_all(key_value, "ctx", split_axis=0, concat_axis=1, tiled=True),
    )
    query_part = query_part[0]
    grad_part = grad_part[0]
    key_value = key_value[0]
    attended, grad_query, key_grads = attend_block(
        query_part, grad_part, key_value, valid_keys, heads_dev
    )
    outgoing = jnp.concatenate([attended, grad_query], axis=1).reshape(
        devices_ctx, part_rows, 2 * block_width
    )
    returned = lax.all_to_all(outgoing, "ctx", split_axis=0, concat_axis=0, tiled=True)
    key_returned = lax.all_to_all(
        key_grads.reshape(devices_ctx, rows_here, 2 * block_width).astype(jnp.bfloat16),
        "ctx",
        split_axis=0,
        concat_axis=0,
        tiled=True,
    ).astype(jnp.float32)
    columns = 2 * block_width
    split = returned.reshape(block_heads, part_count, part_rows, columns).transpose(1, 2, 0, 3)
    returned = split.reshape(rows_here, block_heads, columns)
    attention_out = returned[:, :, :block_width].reshape(rows_here, embed)
    grad_q = returned[:, :, block_width:].reshape(rows_here, embed)
    summed = jnp.sum(
        key_returned.reshape(block_heads, part_count, rows_here, 2 * block_width), axis=1
    )
    summed = summed.astype(jnp.bfloat16).transpose(1, 0, 2)
    grad_k = summed[:, :, :block_width].reshape(rows_here, embed)
    grad_v = summed[:, :, block_width:].reshape(rows_here, embed)
    half_width = KSIZE // 2
    taps = depth_kernel[0]
    bias = depth_bias[0]
    gated = gated_input[0, 0]
    masked = jnp.where(frame_mask[:, None], gated, jnp.zeros((), jnp.bfloat16))
    padded = padded_2(masked, (("ctx", 0),), half_width)
    pre_act = depthwise(padded, taps, bias, rows_here)
    grad_pre = grad_depth.astype(jnp.float32) * slope(pre_act)
    grad_pad = padded_2(grad_pre, (("ctx", 0),), half_width)
    depth_out = (pre_act * jax.nn.sigmoid(pre_act)).astype(jnp.bfloat16)
    back = jnp.zeros((rows_here, taps.shape[1]), jnp.float32)
    for offset in range(KSIZE):
        start = 2 * half_width - offset
        back = back + taps[offset][None, :] * grad_pad[start : start + rows_here]
    gated_grad = jnp.where(frame_mask[:, None], back, 0.0).astype(jnp.bfloat16)
    kernel_local = jnp.stack(
        [
            jnp.sum(padded[offset : offset + rows_here].astype(jnp.float32) * grad_pre, axis=0)
            for offset in range(KSIZE)
        ]
    )
    bias_local = jnp.sum(grad_pre, axis=0)
    kernel_grad, bias_grad = lax.psum((kernel_local, bias_local), ("dp", "ctx"))
    projected_grad = jnp.concatenate([grad_q, grad_k, grad_v], axis=1)
    return (
        attention_out[None, None],
        depth_out[None, None],
        projected_grad[None, None],
        gated_grad[None, None],
        kernel_grad[None],
        bias_grad[None],
    )


def solution(mesh):
    placed = (
        P("pipe", "dp", "ctx", None),
        P("pipe", "dp", "ctx", None),
        P("pipe", "dp", "ctx", None),
        P("pipe", "dp"),
        P("pipe", None, None),
        P("pipe", None),
    )
    return jax.shard_map(
        local,
        mesh=mesh,
        in_specs=placed,
        out_specs=(
            P("pipe", "dp", "ctx", None),
            P("pipe", "dp", "ctx", None),
            P("pipe", "dp", "ctx", None),
            P("pipe", "dp", "ctx", None),
            P("pipe", None, None),
            P("pipe", None),
        ),
        check_vma=False,
    )
```

profile of v0, /device:TPU:0, one launch (start us, length us, event | category | flops | bytes accessed | tf_op | source)
XLA Modules:
  0.0 200.0 jit_solution(13303225998379243030)
XLA Ops:
  7.2 1.4 copy.80
  9.3 4.4 %all-to-all-start = ((bf16[2,128,384]{1,2,0:T(8,128)(2,1)}), bf16[2,128,384]{1,2,0:T(8,128)(2,1)S(1)}, u32[]{:S(2)}, u32[]{:S(2)}) async-start(bf16[2,128,384]{1,2,0:T(8,128)(2,1)} %bitcast.3), calls=%async_computation | async-start | bytes 393216 | tf_op jit(solution)/shard_map/all_to_all | solution.py:152
  13.6 1.1 copy.85
  14.7 1.6 collective-permute-start
  18.7 3.6 %collective-permute-start.1 = (bf16[15,1536]{0,1:T(8,128)(2,1)}, bf16[15,1536]{0,1:T(8,128)(2,1)S(1)}, u32[]{:S(2)}, u32[]{:S(2)}) collective-permute-start(bf16[15,1536]{0,1:T(8,128)(2,1)} %get-tuple-element.278), channel_id=1, source_target_pairs={{0,1},{2,3},{4,5},{6,7},{8,9},{10,11},{12,13},{14,15},{16,17},{18,... | collective-permute-start | bytes 138248 | tf_op jit(solution)/shard_map/ppermute | solution.py:22
  22.4 1.3 collective-permute-start.2
  24.5 3.9 %all-to-all-start.1 = ((bf16[2,128,768]{1,2,0:T(8,128)(2,1)}), bf16[2,128,768]{1,2,0:T(8,128)(2,1)S(1)}, u32[]{:S(2)}, u32[]{:S(2)}) async-start(bf16[2,128,768]{1,2,0:T(8,128)(2,1)} %maximum_bitcast_fusion.1), calls=%async_computation.1 | async-start | bytes 786432 | tf_op jit(solution)/shard_map/all_to_all | solution.py:154
  29.6 9.0 %all-to-all-done.1 = bf16[2,128,768]{1,2,0:T(8,128)(2,1)S(1)} async-done(((bf16[2,128,768]{1,2,0:T(8,128)(2,1)}), bf16[2,128,768]{1,2,0:T(8,128)(2,1)S(1)}, u32[]{:S(2)}, u32[]{:S(2)}) %all-to-all-start.1) | async-done | bytes 393248 | tf_op jit(solution)/shard_map/all_to_all | solution.py:154
  39.8 0.9 slice.581
  41.6 4.1 %all-to-all-start.2 = ((bf16[2,128,384]{2,1,0:T(8,128)(2,1)}), bf16[2,128,384]{2,1,0:T(8,128)(2,1)}, u32[]{:S(2)}, u32[]{:S(2)}) async-start(bf16[2,128,384]{2,1,0:T(8,128)(2,1)} %copy.86), calls=%async_computation.2 | async-start | bytes 393216 | tf_op jit(solution)/shard_map/all_to_all | solution.py:153
  46.2 18.7 %fusion.95 = (f32[1536]{0:T(1024)S(1)}, f32[1536]{0:T(1024)S(1)}, f32[1536]{0:T(1024)S(1)}, f32[1536]{0:T(1024)S(1)}, f32[1536]{0:T(1024)S(1)}, /*index=5*/f32[1...) fusion(bf16[15,1536]{0,1:T(8,128)(2,1)S(1)} %collective-permute, ...), kind=kLoop, calls=%fused_computation.278 | loop fusion | flops 47565312 | bytes 2703360 | tf_op jit(solution)/shard_map/reduce_sum | solution.py:201
  65.0 1.1 fusion.220
  66.1 3.0 %fusion.80 = (f32[1536]{0:T(1024)S(1)}, f32[1536]{0:T(1024)S(1)}, f32[1536]{0:T(1024)S(1)}, f32[1536]{0:T(1024)S(1)}, f32[1536]{0:T(1024)S(1)}, /*index=5*/f32[1536]{0:T(1024)S(1)}, f32[1536]{0:T(1024)S(1)}, f32[1536]{0:T(1024)S(1)}) fusion(f32[128,1536]{0,1:T(8,128)S(1)} %get-tuple-element.263, bf16[15,1536]{0,1:T(8,128)(2,1)S(1)} %copy-done.2, ...), kind=kLoop, calls=%fused_computation.263 | loop fusion | flops 7852032 | bytes 1274880 | tf_op jit(solution)/shard_map/reduce_sum | solution.py:201
  79.3 3.8 %fusion.73 = (f32[1536]{0:T(1024)S(1)}, f32[1536]{0:T(1024)S(1)}, f32[1536]{0:T(1024)S(1)}, f32[1536]{0:T(1024)S(1)}, f32[1536]{0:T(1024)S(1)}, /*index=5*/f32[1...) fusion(f32[128,1536]{0,1:T(8,128)S(1)} %get-tuple-element.263, ...), kind=kLoop, calls=%fused_computation.256 | loop fusion | flops 10603008 | bytes 1281024 | tf_op jit(solution)/shard_map/reduce_sum | solution.py:201
  83.7 2.5 %fusion.64 = (f32[1536]{0:T(1024)S(1)}, f32[1536]{0:T(1024)S(1)}, f32[1536]{0:T(1024)S(1)}, f32[1536]{0:T(1024)S(1)}, f32[1536]{0:T(1024)S(1)}, /*index=5*/f32[1536]{0:T(1024)S(1)}) fusion(f32[128,1536]{0,1:T(8,128)S(1)} %get-tuple-element.263, bf16[128,1536]{0,1:T(8,128)(2,1)S(1)} %bitcast_select_fusion, bf16[15,1536]{0,1:T(8,128)(2,1)S(1)} %collective-permute-done.1), kind=kLoop, calls=%fused_computation.247 | loop fusion | flops 7068672 | bytes 1262592 | tf_op jit(solution)/shard_map/reduce_sum | solution.py:201
  94.6 6.0 %stack.127 = f32[31,1536]{1,0:T(8,128)} concatenate(f32[1,1536]{1,0:T(1,128)} %stack.96, f32[1,1536]{1,0:T(1,128)} %stack.97, f32[1,1536]{1,0:T(1,128)} %stack.98, f32[1,1536]{1,0:T(1,128)} %stack.99, f32[1,1536]{1,0:T(1,128)} %stack.100, f32[1,1536]{1,0:T(1,128)} %stack.101, f32[1,1536]{1,0:T(1,128)} %stack.102, f32[1,1536]{1,0:T(1,128)} %stack.103, f32[1,1536]{1,0:T(1,128)} %stack.104, ...), dimensions={0} | concatenate | bytes 380928 | tf_op jit(solution)/shard_map/stack | solution.py:199
  100.5 1.7 broadcast_in_dim.88
  104.1 3.7 %collective-permute-start.4 = (f32[15,1536]{1,0:T(8,128)}, f32[15,1536]{1,0:T(8,128)S(1)}, u32[]{:S(2)}, u32[]{:S(2)}) collective-permute-start(f32[15,1536]{1,0:T(8,128)} %copy.98), channel_id=1, source_target_pairs={{0,1},{2,3},{4,5},{6,7},{8,9},{10,11},{12,13},{14,15},{16,17},{18,... | collective-permute-start | bytes 276488 | tf_op jit(solution)/shard_map/ppermute | solution.py:22
  107.8 1.3 collective-permute-start.3
  110.2 24.2 %psum.15 = f32[1,1536]{1,0:T(1,128)} all-reduce(f32[1,1536]{1,0:T(1,128)S(1)} %copy-done.65), channel_id=1, replica_groups=mesh['dp'=4,'pipe'=4,'ctx'=2] {'dp','ctx'}, use_global_device_ids=true, to_apply=%region_38.39 | all-reduce | flops 1536 | bytes 12288 | tf_op jit(solution)/shard_map/psum | solution.py:206
  135.1 1.1 copy.87
  136.3 13.2 %while.17 = (s32[]{:T(128)}, bf16[4,256,96]{1,2,0:T(8,128)(2,1)}, bf16[4,256,96]{1,2,0:T(8,128)(2,1)}, bf16[4,256,96]{1,2,0:T(8,128)(2,1)}, bf16[4,256,96]{1,2,0...) while((s32[]{:T(128)}, bf16[4,256,96]{1,2,0:T(8,128)(2,1)}, ...), condition=%wide.region_4.5_spmd.clone, body=%wide.region_0.4_spmd.clone.sunk | while | flops 76471808 | bytes 4224949 | solution.py:98
  149.5 1.0 concatenate.94
  150.5 1.0 concatenate.95
  152.2 1.0 copy.91
  153.3 3.7 %all-to-all-start.3 = ((bf16[2,128,768]{2,1,0:T(8,128)(2,1)}), bf16[2,128,768]{2,1,0:T(8,128)(2,1)S(1)}, u32[]{:S(2)}, u32[]{:S(2)}) async-start(bf16[2,128,768]{2,1,0:T(8,128)(2,1)} %copy.91), calls=%async_computation.3 | async-start | bytes 786432 | tf_op jit(solution)/shard_map/all_to_all | solution.py:165
  157.2 21.0 %fusion.217 = bf16[1,1,128,1536]{2,3,1,0:T(8,128)(2,1)S(1)} fusion(f32[128,1536]{0,1:T(8,128)S(1)} %get-tuple-element.263, f32[15,1536]{0,1:T(8,128)S(1)} %copy.99, f32[1536]{0:T(1024)} %copy-done.63, f32[1536]{0:T(1024)} %copy-done.64, f32[1536]{0:T(1024)S(1)} %get-tuple-element.213, f32[1536]{0:T(1024)S(1)} %copy-done.13, f32[1536]{0:T(1024)S(1)} %copy-done.15, ...), kind=kLoop, calls=%fused_computation.411 | loop fusion | flops 18284544 | bytes 1554560 | tf_op jit(solution)/shard_map/broadcast_in_dim | solution.py:212
  179.8 1.0 copy.94
  180.9 3.5 %all-to-all-start.4 = ((bf16[2,128,768]{2,1,0:T(8,128)(2,1)}), bf16[2,128,768]{2,1,0:T(8,128)(2,1)S(1)}, u32[]{:S(2)}, u32[]{:S(2)}) async-start(bf16[2,128,768]{2,1,0:T(8,128)(2,1)} %copy.94), calls=%async_computation.4 | async-start | bytes 786432 | tf_op jit(solution)/shard_map/all_to_all | solution.py:166
  185.4 4.8 %all-to-all-done.4 = bf16[2,128,768]{2,1,0:T(8,128)(2,1)S(1)} async-done(((bf16[2,128,768]{2,1,0:T(8,128)(2,1)}), bf16[2,128,768]{2,1,0:T(8,128)(2,1)S(1)}, u32[]{:S(2)}, u32[]{:S(2)}) %all-to-all-start.4) | async-done | bytes 393248 | tf_op jit(solution)/shard_map/all_to_all | solution.py:166
  190.5 1.1 copy.102
  191.6 1.6 copy.131
  (269 shorter events, 45.6 us)
Async XLA Ops:
  9.3 15.3 %all-to-all-start = ((bf16[2,128,384]{1,2,0:T(8,128)(2,1)}), bf16[2,128,384]{1,2,0:T(8,128)(2,1)S(1)}, u32[]{:S(2)}, u32[]{:S(2)}) async-start(bf16[2,128,384]{1,2,0:T(8,128)(2,1)} %bitcast.3), calls=%async_computation | async-start | bytes 393216 | tf_op jit(solution)/shard_map/all_to_all | solution.py:152
  14.7 25.1 %collective-permute-start = (bf16[1,1,128,2304]{2,3,1,0:T(8,128)(2,1)}, bf16[1,1,128,2304]{2,3,1,0:T(8,128)(2,1)}, u32[]{:S(2)}, u32[]{:S(2)}) collective-permute-start(bf16[1,1,128,2304]{2,3,1,0:T(8,128)(2,1)} %copy.85), channel_id=1, source_target_pairs={{0,6},{2,0},{4,2},{6,4},{1,7},{3,1},{5,3},{7,5},{8,14},{10,8},{12,... | collective-permute-start | bytes 1769480 | tf_op jit(solution)/shard_map/ppermute | solution.py:14
  18.7 27.2 %collective-permute-start.1 = (bf16[15,1536]{0,1:T(8,128)(2,1)}, bf16[15,1536]{0,1:T(8,128)(2,1)S(1)}, u32[]{:S(2)}, u32[]{:S(2)}) collective-permute-start(bf16[15,1536]{0,1:T(8,128)(2,1)} %get-tuple-element.278), channel_id=1, source_target_pairs={{0,1},{2,3},{4,5},{6,7},{8,9},{10,11},{12,13},{14,15},{16,17},{18,... | collective-permute-start | bytes 138248 | tf_op jit(solution)/shard_map/ppermute | solution.py:22
  22.4 23.5 %collective-permute-start.2 = (bf16[15,1536]{0,1:T(8,128)(2,1)S(1)}, bf16[15,1536]{0,1:T(8,128)(2,1)S(1)}, u32[]{:S(2)}, u32[]{:S(2)}) collective-permute-start(bf16[15,1536]{0,1:T(8,128)(2,1)S(1)} %get-tuple-element.279), channel_id=1, source_target_pairs={{1,0},{3,2},{5,4},{7,6},{9,8},{11,10},{13,12},{15,14},{17,16},{19,... | collective-permute-start | bytes 138248 | tf_op jit(solution)/shard_map/ppermute | solution.py:25
  24.5 14.1 %all-to-all-start.1 = ((bf16[2,128,768]{1,2,0:T(8,128)(2,1)}), bf16[2,128,768]{1,2,0:T(8,128)(2,1)S(1)}, u32[]{:S(2)}, u32[]{:S(2)}) async-start(bf16[2,128,768]{1,2,0:T(8,128)(2,1)} %maximum_bitcast_fusion.1), calls=%async_computation.1 | async-start | bytes 786432 | tf_op jit(solution)/shard_map/all_to_all | solution.py:154
  28.6 17.3 %copy-start.46 = (f32[1536]{0:T(1024)}, f32[1536]{0:T(1024)S(1)}, u32[]{:S(2)}) copy-start(f32[1536]{0:T(1024)S(1)} %get-tuple-element.231) | copy-start | bytes 18436
  28.7 17.3 %copy-start.48 = (f32[1536]{0:T(1024)}, f32[1536]{0:T(1024)S(1)}, u32[]{:S(2)}) copy-start(f32[1536]{0:T(1024)S(1)} %get-tuple-element.232) | copy-start | bytes 18436
  28.7 17.3 %copy-start.50 = (f32[1536]{0:T(1024)}, f32[1536]{0:T(1024)S(1)}, u32[]{:S(2)}) copy-start(f32[1536]{0:T(1024)S(1)} %get-tuple-element.233) | copy-start | bytes 18436
  28.7 17.3 %copy-start.52 = (f32[1536]{0:T(1024)}, f32[1536]{0:T(1024)S(1)}, u32[]{:S(2)}) copy-start(f32[1536]{0:T(1024)S(1)} %get-tuple-element.234) | copy-start | bytes 18436
  28.7 17.3 %copy-start.54 = (f32[1536]{0:T(1024)}, f32[1536]{0:T(1024)S(1)}, u32[]{:S(2)}) copy-start(f32[1536]{0:T(1024)S(1)} %get-tuple-element.235) | copy-start | bytes 18436
  28.7 17.3 %copy-start.56 = (f32[1536]{0:T(1024)}, f32[1536]{0:T(1024)S(1)}, u32[]{:S(2)}) copy-start(f32[1536]{0:T(1024)S(1)} %get-tuple-element.236) | copy-start | bytes 18436
  28.7 17.3 %copy-start.58 = (f32[1536]{0:T(1024)}, f32[1536]{0:T(1024)S(1)}, u32[]{:S(2)}) copy-start(f32[1536]{0:T(1024)S(1)} %get-tuple-element.237) | copy-start | bytes 18436
  28.7 17.3 %copy-start.60 = (f32[1536]{0:T(1024)}, f32[1536]{0:T(1024)S(1)}, u32[]{:S(2)}) copy-start(f32[1536]{0:T(1024)S(1)} %get-tuple-element.238) | copy-start | bytes 18436
  28.7 17.3 %copy-start.61 = (f32[1536]{0:T(1024)}, f32[1536]{0:T(1024)S(1)}, u32[]{:S(2)}) copy-start(f32[1536]{0:T(1024)S(1)} %get-tuple-element.239) | copy-start | bytes 18436
  28.7 17.3 %copy-start.62 = (f32[1536]{0:T(1024)}, f32[1536]{0:T(1024)S(1)}, u32[]{:S(2)}) copy-start(f32[1536]{0:T(1024)S(1)} %get-tuple-element.240) | copy-start | bytes 18436
  28.7 17.3 %copy-start.63 = (f32[1536]{0:T(1024)}, f32[1536]{0:T(1024)S(1)}, u32[]{:S(2)}) copy-start(f32[1536]{0:T(1024)S(1)} %get-tuple-element.241) | copy-start | bytes 18436
  28.8 17.3 %copy-start.64 = (f32[1536]{0:T(1024)}, f32[1536]{0:T(1024)S(1)}, u32[]{:S(2)}) copy-start(f32[1536]{0:T(1024)S(1)} %get-tuple-element.242) | copy-start | bytes 18436
  29.1 17.0 %copy-start.12 = (f32[1536]{0:T(1024)}, f32[1536]{0:T(1024)S(1)}, u32[]{:S(2)}) copy-start(f32[1536]{0:T(1024)S(1)} %get-tuple-element.214) | copy-start | bytes 18436
  29.1 17.0 %copy-start.14 = (f32[1536]{0:T(1024)}, f32[1536]{0:T(1024)S(1)}, u32[]{:S(2)}) copy-start(f32[1536]{0:T(1024)S(1)} %get-tuple-element.215) | copy-start | bytes 18436
  29.1 17.0 %copy-start.16 = (f32[1536]{0:T(1024)}, f32[1536]{0:T(1024)S(1)}, u32[]{:S(2)}) copy-start(f32[1536]{0:T(1024)S(1)} %get-tuple-element.216) | copy-start | bytes 18436
  29.1 17.0 %copy-start.18 = (f32[1536]{0:T(1024)}, f32[1536]{0:T(1024)S(1)}, u32[]{:S(2)}) copy-start(f32[1536]{0:T(1024)S(1)} %get-tuple-element.217) | copy-start | bytes 18436
  29.1 17.0 %copy-start.20 = (f32[1536]{0:T(1024)}, f32[1536]{0:T(1024)S(1)}, u32[]{:S(2)}) copy-start(f32[1536]{0:T(1024)S(1)} %get-tuple-element.218) | copy-start | bytes 18436
  29.1 17.0 %copy-start.22 = (f32[1536]{0:T(1024)}, f32[1536]{0:T(1024)S(1)}, u32[]{:S(2)}) copy-start(f32[1536]{0:T(1024)S(1)} %get-tuple-element.219) | copy-start | bytes 18436
  29.1 17.0 %copy-start.24 = (f32[1536]{0:T(1024)}, f32[1536]{0:T(1024)S(1)}, u32[]{:S(2)}) copy-start(f32[1536]{0:T(1024)S(1)} %get-tuple-element.220) | copy-start | bytes 18436
  29.1 17.0 %copy-start.26 = (f32[1536]{0:T(1024)}, f32[1536]{0:T(1024)S(1)}, u32[]{:S(2)}) copy-start(f32[1536]{0:T(1024)S(1)} %get-tuple-element.221) | copy-start | bytes 18436
  41.6 93.5 %all-to-all-start.2 = ((bf16[2,128,384]{2,1,0:T(8,128)(2,1)}), bf16[2,128,384]{2,1,0:T(8,128)(2,1)}, u32[]{:S(2)}, u32[]{:S(2)}) async-start(bf16[2,128,384]{2,1,0:T(8,128)(2,1)} %copy.86), calls=%async_computation.2 | async-start | bytes 393216 | tf_op jit(solution)/shard_map/all_to_all | solution.py:153
  45.7 145.9 %all-reduce.2.cloned.1.call-start = ((), (), s32[]{:S(2)}) async-start(), calls=%async_computation.5 | async-start | bytes 380928 | tf_op jit(solution)/shard_map/psum | solution.py:206
  45.9 19.1 %copy-start.1 = (bf16[15,1536]{0,1:T(8,128)(2,1)}, bf16[15,1536]{0,1:T(8,128)(2,1)S(1)}, u32[]{:S(2)}) copy-start(bf16[15,1536]{0,1:T(8,128)(2,1)S(1)} %collective-permute-done.2) | copy-start | bytes 138244
  104.1 30.7 %collective-permute-start.4 = (f32[15,1536]{1,0:T(8,128)}, f32[15,1536]{1,0:T(8,128)S(1)}, u32[]{:S(2)}, u32[]{:S(2)}) collective-permute-start(f32[15,1536]{1,0:T(8,128)} %copy.98), channel_id=1, source_target_pairs={{0,1},{2,3},{4,5},{6,7},{8,9},{10,11},{12,13},{14,15},{16,17},{18,... | collective-permute-start | bytes 276488 | tf_op jit(solution)/shard_map/ppermute | solution.py:22
  107.8 26.7 %collective-permute-start.3 = (f32[15,1536]{1,0:T(8,128)S(1)}, f32[15,1536]{1,0:T(8,128)S(1)}, u32[]{:S(2)}, u32[]{:S(2)}) collective-permute-start(f32[15,1536]{1,0:T(8,128)S(1)} %copy-done.11), channel_id=1, source_target_pairs={{1,0},{3,2},{5,4},{7,6},{9,8},{11,10},{13,12},{15,14},{17,16},{19,... | collective-permute-start | bytes 276488 | tf_op jit(solution)/shard_map/ppermute | solution.py:25
  153.3 27.6 %all-to-all-start.3 = ((bf16[2,128,768]{2,1,0:T(8,128)(2,1)}), bf16[2,128,768]{2,1,0:T(8,128)(2,1)S(1)}, u32[]{:S(2)}, u32[]{:S(2)}) async-start(bf16[2,128,768]{2,1,0:T(8,128)(2,1)} %copy.91), calls=%async_computation.3 | async-start | bytes 786432 | tf_op jit(solution)/shard_map/all_to_all | solution.py:165
  180.9 9.3 %all-to-all-start.4 = ((bf16[2,128,768]{2,1,0:T(8,128)(2,1)}), bf16[2,128,768]{2,1,0:T(8,128)(2,1)S(1)}, u32[]{:S(2)}, u32[]{:S(2)}) async-start(bf16[2,128,768]{2,1,0:T(8,128)(2,1)} %copy.94), calls=%async_computation.4 | async-start | bytes 786432 | tf_op jit(solution)/shard_map/all_to_all | solution.py:166
  (53 other events, 331.8 us)
Sparse Core Ops, SparseCore 0:
  102.4 72.1 all-reduce.1
where the time goes:
time: 201 us; the launch traced here: 200 us
  other arithmetic  54.4 us (27%)
  local copies, waits for them, and re-layouts  50.4 us (25%)
  starting transfers between devices  31.2 us (16%)
  blocking collectives  24.2 us (12%)
  between operations  16 us (8%)
  waiting for transfers between devices  13.8 us (7%)
  matrix products  9.53 us (5%)
    reduce_sum x4, other arithmetic, local(): jnp.sum(padded[offset:offset + rows_here].astype(jnp.float32) * grad_pre,...  28.1 us
    another operation x32, local copies, waits for them, and re-layouts, local(): jnp.stack([jnp.sum(padded[offset:offset + rows_here].astype(jnp.float32)...  24.4 us
    psum x1, blocking collectives, local(): kernel_grad, bias_grad = lax.psum((kernel_local, bias_local), ('dp', 'ctx'))  24.2 us
    broadcast_in_dim x1, other arithmetic, local(): gated_grad[None, None]  21 us
    all_to_all x1, waiting for transfers between devices, local(): lax.all_to_all(key_value, 'ctx', split_axis=0, concat_axis=1, tiled=True)  8.99 us
    unnamed x140, local copies, waits for them, and re-layouts  8.85 us
    ppermute x2, starting transfers between devices, padded_2(): lax.ppermute(lax.slice_in_dim(block, block.shape[dim] - width, None, axis...  7.3 us
    all_to_all x1, waiting for transfers between devices, local(): lax.all_to_all(key_grads.reshape(devices_ctx, rows_here, 2 * block_width)...  4.77 us
  transfers between devices with their start and end apart: 11, of which 2 were waited for; matrix products, arithmetic and copies ran while one was open for 55% of the time, Pallas kernels for 0%

commit v1 on v0

--- a/solution.py
+++ b/solution.py
@@ -203,7 +203,7 @@
         ]
     )
     bias_local = jnp.sum(grad_pre, axis=0)
-    kernel_grad, bias_grad = lax.psum((kernel_local, bias_local), ("dp", "ctx"))
+    kernel_grad, bias_grad = lax.psum(lax.psum((kernel_local, bias_local), "ctx"), "dp")
     projected_grad = jnp.concatenate([grad_q, grad_k, grad_v], axis=1)
     return (
         attention_out[None, None],

time: 201 us -> 220 us (1.095)
  waiting for transfers between devices: 13.8 us -> 37.1 us
  blocking collectives: 24.2 us -> 19 us
  matrix products: 9.53 us -> 12.1 us
    psum x1 -> x2, waiting for transfers between devices: 0.01 us -> 22.8 us  [the longest x1 22.8 us: local(): lax.psum(lax.psum((kernel_local, bias_local), 'ctx'), 'dp')]
    psum x1 -> x2, blocking collectives: 24.2 us -> 19 us  [the longest x1 13.1 us: local(): lax.psum(lax.psum((kernel_local, bias_local), 'ctx'), 'dp')]
    dot_general x4, matrix products: 0.64 us -> 3.25 us  [advance(): lax.dot_general(probs_bf, grad_block, downward, preferred_element_type=jn...]
    dot_general x4, matrix products: 0.67 us -> 3.26 us  [advance(): lax.dot_general(grad_scores, query_block, downward, preferred_element_typ...]
    dot_general x4, matrix products: 3.13 us -> 0.55 us  [advance(): jnp.dot(grad_scores, keys_in, preferred_element_type=jnp.float32)]
    unnamed x140 -> x154, local copies, waits for them, and re-layouts: 8.85 us -> 8.09 us
  transfers between devices with their start and end apart: 11 -> 12, of which waited for: 2 -> 3; matrix products, arithmetic and copies ran while one was open for 55% -> 51% of each run, Pallas kernels for 0% -> 0%
where the time goes in v1:
time: 220 us; the launch traced here: 219 us
  other arithmetic  53.8 us (24%)
  local copies, waits for them, and re-layouts  49.4 us (22%)
  waiting for transfers between devices  37.1 us (17%)
  starting transfers between devices  31.6 us (14%)
  blocking collectives  19 us (9%)
  between operations  16.1 us (7%)
  matrix products  12.1 us (6%)
    reduce_sum x4, other arithmetic, local(): jnp.sum(padded[offset:offset + rows_here].astype(jnp.float32) * grad_pre,...  28.7 us
    another operation x32, local copies, waits for them, and re-layouts, local(): jnp.stack([jnp.sum(padded[offset:offset + rows_here].astype(jnp.float32)...  24.4 us
    psum x1, waiting for transfers between devices, local(): lax.psum(lax.psum((kernel_local, bias_local), 'ctx'), 'dp')  22.8 us
    broadcast_in_dim x1, other arithmetic, local(): gated_grad[None, None]  19.7 us
    psum x1, blocking collectives, local(): lax.psum(lax.psum((kernel_local, bias_local), 'ctx'), 'dp')  13.1 us
    all_to_all x1, waiting for transfers between devices, local(): lax.all_to_all(key_value, 'ctx', split_axis=0, concat_axis=1, tiled=True)  9.2 us
    unnamed x154, local copies, waits for them, and re-layouts  8.09 us
    ppermute x2, starting transfers between devices, padded_2(): lax.ppermute(lax.slice_in_dim(block, block.shape[dim] - width, None, axis...  7.49 us
  transfers between devices with their start and end apart: 12, of which 3 were waited for; matrix products, arithmetic and copies ran while one was open for 51% of the time, Pallas kernels for 0%

profile of v1, /device:TPU:0, one launch (start us, length us, event | category | flops | bytes accessed | tf_op | source)
XLA Modules:
  0.0 219.3 jit_solution(17262016638508330)
XLA Ops:
  7.2 1.4 copy.80
  9.3 4.4 %all-to-all-start = ((bf16[2,128,384]{1,2,0:T(8,128)(2,1)}), bf16[2,128,384]{1,2,0:T(8,128)(2,1)S(1)}, u32[]{:S(2)}, u32[]{:S(2)}) async-start(bf16[2,128,384]{1,2,0:T(8,128)(2,1)} %bitcast.3), calls=%async_computation | async-start | bytes 393216 | tf_op jit(solution)/shard_map/all_to_all | solution.py:152
  13.9 1.6 collective-permute-start
  17.0 1.0 fusion.224
  18.0 3.6 %collective-permute-start.1 = (bf16[15,1536]{0,1:T(8,128)(2,1)}, bf16[15,1536]{0,1:T(8,128)(2,1)S(1)}, u32[]{:S(2)}, u32[]{:S(2)}) collective-permute-start(bf16[15,1536]{0,1:T(8,128)(2,1)} %get-tuple-element.278), channel_id=1, source_target_pairs={{0,1},{2,3},{4,5},{6,7},{8,9},{10,11},{12,13},{14,15},{16,17},{18,... | collective-permute-start | bytes 138248 | tf_op jit(solution)/shard_map/ppermute | solution.py:22
  21.7 1.3 collective-permute-start.2
  23.9 3.9 %all-to-all-start.1 = ((bf16[2,128,768]{1,2,0:T(8,128)(2,1)}), bf16[2,128,768]{1,2,0:T(8,128)(2,1)S(1)}, u32[]{:S(2)}, u32[]{:S(2)}) async-start(bf16[2,128,768]{1,2,0:T(8,128)(2,1)} %maximum_bitcast_fusion.1), calls=%async_computation.1 | async-start | bytes 786432 | tf_op jit(solution)/shard_map/all_to_all | solution.py:154
  28.9 9.2 %all-to-all-done.1 = bf16[2,128,768]{1,2,0:T(8,128)(2,1)S(1)} async-done(((bf16[2,128,768]{1,2,0:T(8,128)(2,1)}), bf16[2,128,768]{1,2,0:T(8,128)(2,1)S(1)}, u32[]{:S(2)}, u32[]{:S(2)}) %all-to-all-start.1) | async-done | bytes 393248 | tf_op jit(solution)/shard_map/all_to_all | solution.py:154
  41.1 4.1 %all-to-all-start.2 = ((bf16[2,128,384]{2,1,0:T(8,128)(2,1)}), bf16[2,128,384]{2,1,0:T(8,128)(2,1)}, u32[]{:S(2)}, u32[]{:S(2)}) async-start(bf16[2,128,384]{2,1,0:T(8,128)(2,1)} %copy.86), calls=%async_computation.2 | async-start | bytes 393216 | tf_op jit(solution)/shard_map/all_to_all | solution.py:153
  45.6 18.7 %fusion.95 = (f32[1536]{0:T(1024)S(1)}, f32[1536]{0:T(1024)S(1)}, f32[1536]{0:T(1024)S(1)}, f32[1536]{0:T(1024)S(1)}, f32[1536]{0:T(1024)S(1)}, /*index=5*/f32[1...) fusion(bf16[15,1536]{0,1:T(8,128)(2,1)S(1)} %collective-permute, ...), kind=kLoop, calls=%fused_computation.278 | loop fusion | flops 47565312 | bytes 2703360 | tf_op jit(solution)/shard_map/reduce_sum | solution.py:201
  64.3 1.1 fusion.220
  65.5 3.6 %fusion.80 = (f32[1536]{0:T(1024)S(1)}, f32[1536]{0:T(1024)S(1)}, f32[1536]{0:T(1024)S(1)}, f32[1536]{0:T(1024)S(1)}, f32[1536]{0:T(1024)S(1)}, /*index=5*/f32[1536]{0:T(1024)S(1)}, f32[1536]{0:T(1024)S(1)}, f32[1536]{0:T(1024)}) fusion(f32[128,1536]{0,1:T(8,128)S(1)} %get-tuple-element.263, bf16[15,1536]{0,1:T(8,128)(2,1)S(1)} %copy-done.2, ...), kind=kLoop, calls=%fused_computation.263 | loop fusion | flops 7852032 | bytes 1274880 | tf_op jit(solution)/shard_map/reduce_sum | solution.py:201
  78.6 5.9 %psum.30 = f32[1536]{0:T(1024)} all-reduce(f32[1536]{0:T(1024)} %get-tuple-element.211), channel_id=1, replica_groups=mesh['dp'=4,'pipe'=4,'ctx'=2] {'ctx'}, use_global_device_ids=true, to_apply=%region_39.40 | all-reduce | flops 1536 | bytes 12288 | tf_op jit(solution)/shard_map/psum | solution.py:206
  84.5 1.3 broadcast_in_dim.89
  85.8 3.8 %fusion.73 = (f32[1536]{0:T(1024)S(1)}, f32[1536]{0:T(1024)S(1)}, f32[1536]{0:T(1024)S(1)}, f32[1536]{0:T(1024)S(1)}, f32[1536]{0:T(1024)S(1)}, /*index=5*/f32[1...) fusion(f32[128,1536]{0,1:T(8,128)S(1)} %get-tuple-element.263, ...), kind=kLoop, calls=%fused_computation.256 | loop fusion | flops 10603008 | bytes 1281024 | tf_op jit(solution)/shard_map/reduce_sum | solution.py:201
  90.2 2.5 %fusion.64 = (f32[1536]{0:T(1024)S(1)}, f32[1536]{0:T(1024)S(1)}, f32[1536]{0:T(1024)S(1)}, f32[1536]{0:T(1024)S(1)}, f32[1536]{0:T(1024)S(1)}, /*index=5*/f32[1536]{0:T(1024)S(1)}) fusion(f32[128,1536]{0,1:T(8,128)S(1)} %get-tuple-element.263, bf16[128,1536]{0,1:T(8,128)(2,1)S(1)} %bitcast_select_fusion, bf16[15,1536]{0,1:T(8,128)(2,1)S(1)} %collective-permute-done.1), kind=kLoop, calls=%fused_computation.247 | loop fusion | flops 7068672 | bytes 1262592 | tf_op jit(solution)/shard_map/reduce_sum | solution.py:201
  101.1 5.9 %stack.127 = f32[31,1536]{1,0:T(8,128)} concatenate(f32[1,1536]{1,0:T(1,128)} %stack.96, f32[1,1536]{1,0:T(1,128)} %stack.97, f32[1,1536]{1,0:T(1,128)} %stack.98, f32[1,1536]{1,0:T(1,128)} %stack.99, f32[1,1536]{1,0:T(1,128)} %stack.100, f32[1,1536]{1,0:T(1,128)} %stack.101, f32[1,1536]{1,0:T(1,128)} %stack.102, f32[1,1536]{1,0:T(1,128)} %stack.103, f32[1,1536]{1,0:T(1,128)} %stack.104, ...), dimensions={0} | concatenate | bytes 380928 | tf_op jit(solution)/shard_map/stack | solution.py:199
  108.9 3.9 %collective-permute-start.4 = (f32[15,1536]{1,0:T(8,128)}, f32[15,1536]{1,0:T(8,128)S(1)}, u32[]{:S(2)}, u32[]{:S(2)}) collective-permute-start(f32[15,1536]{1,0:T(8,128)} %copy.98), channel_id=1, source_target_pairs={{0,1},{2,3},{4,5},{6,7},{8,9},{10,11},{12,13},{14,15},{16,17},{18,... | collective-permute-start | bytes 276488 | tf_op jit(solution)/shard_map/ppermute | solution.py:22
  112.7 1.3 collective-permute-start.3
  115.2 13.1 %psum.31 = f32[1,1536]{1,0:T(1,128)} all-reduce(f32[1,1536]{1,0:T(1,128)S(1)} %copy-done.69), channel_id=1, replica_groups=mesh['dp'=4,'pipe'=4,'ctx'=2] {'dp'}, use_global_device_ids=true, to_apply=%region_40.41 | all-reduce | flops 1536 | bytes 12288 | tf_op jit(solution)/shard_map/psum | solution.py:206
  129.0 1.1 copy.87
  130.2 15.5 %while.17 = (s32[]{:T(128)}, bf16[4,256,96]{1,2,0:T(8,128)(2,1)}, bf16[4,256,96]{1,2,0:T(8,128)(2,1)S(1)}, bf16[4,256,96]{1,2,0:T(8,128)(2,1)}, bf16[4,256,96]{1...) while((s32[]{:T(128)}, bf16[4,256,96]{1,2,0:T(8,128)(2,1)}, ...), condition=%wide.region_4.5_spmd.clone, body=%wide.region_0.4_spmd.clone.sunk | while | flops 76471808 | bytes 2652029 | solution.py:98
  147.6 1.0 copy.91
  148.7 3.9 %all-to-all-start.3 = ((bf16[2,128,768]{2,1,0:T(8,128)(2,1)}), bf16[2,128,768]{2,1,0:T(8,128)(2,1)S(1)}, u32[]{:S(2)}, u32[]{:S(2)}) async-start(bf16[2,128,768]{2,1,0:T(8,128)(2,1)} %copy.91), calls=%async_computation.3 | async-start | bytes 786432 | tf_op jit(solution)/shard_map/all_to_all | solution.py:165
  152.9 19.7 %fusion.217 = bf16[1,1,128,1536]{2,3,1,0:T(8,128)(2,1)S(1)} fusion(f32[128,1536]{0,1:T(8,128)S(1)} %get-tuple-element.263, f32[15,1536]{0,1:T(8,128)S(1)} %copy.99, f32[1536]{0:T(1024)S(1)} %copy-done.66, f32[1536]{0:T(1024)S(1)} %copy-done.68, f32[1536]{0:T(1024)S(1)} %get-tuple-element.213, f32[1536]{0:T(1024)S(1)} %copy-done.12, f32[1536]{0:T(1024)S(1)} %copy-done.14, ...), kind=kLoop, calls=%fused_computation.411 | loop fusion | flops 18284544 | bytes 1554560 | tf_op jit(solution)/shard_map/broadcast_in_dim | solution.py:212
  174.2 1.0 copy.94
  175.2 1.7 broadcast_in_dim.88
  177.0 3.5 %all-to-all-start.4 = ((bf16[2,128,768]{2,1,0:T(8,128)(2,1)}), bf16[2,128,768]{2,1,0:T(8,128)(2,1)S(1)}, u32[]{:S(2)}, u32[]{:S(2)}) async-start(bf16[2,128,768]{2,1,0:T(8,128)(2,1)} %copy.94), calls=%async_computation.4 | async-start | bytes 786432 | tf_op jit(solution)/shard_map/all_to_all | solution.py:166
  181.6 5.0 %all-to-all-done.4 = bf16[2,128,768]{2,1,0:T(8,128)(2,1)S(1)} async-done(((bf16[2,128,768]{2,1,0:T(8,128)(2,1)}), bf16[2,128,768]{2,1,0:T(8,128)(2,1)S(1)}, u32[]{:S(2)}, u32[]{:S(2)}) %all-to-all-start.4) | async-done | bytes 393248 | tf_op jit(solution)/shard_map/all_to_all | solution.py:166
  186.9 1.1 copy.102
  188.0 22.8 %all-reduce.5.cloned.1.call-done = f32[1,31,1536]{2,0,1:T(1,128)} async-done(((f32[1,31,1536]{2,0,1:T(1,128)}), f32[1,31,1536]{2,0,1:T(1,128)}) %all-reduce.5.cloned.1.call-update) | async-done | bytes 190480 | tf_op jit(solution)/shard_map/psum | solution.py:206
  210.8 1.6 copy.132
  (271 shorter events, 48.7 us)
Async XLA Ops:
  9.3 14.6 %all-to-all-start = ((bf16[2,128,384]{1,2,0:T(8,128)(2,1)}), bf16[2,128,384]{1,2,0:T(8,128)(2,1)S(1)}, u32[]{:S(2)}, u32[]{:S(2)}) async-start(bf16[2,128,384]{1,2,0:T(8,128)(2,1)} %bitcast.3), calls=%async_computation | async-start | bytes 393216 | tf_op jit(solution)/shard_map/all_to_all | solution.py:152
  13.9 25.4 %collective-permute-start = (bf16[1,1,128,2304]{2,3,1,0:T(8,128)(2,1)S(1)}, bf16[1,1,128,2304]{2,3,1,0:T(8,128)(2,1)}, u32[]{:S(2)}, u32[]{:S(2)}) collective-permute-start(bf16[1,1,128,2304]{2,3,1,0:T(8,128)(2,1)S(1)} %copy.85), channel_id=1, source_target_pairs={{0,6},{2,0},{4,2},{6,4},{1,7},{3,1},{5,3},{7,5},{8,14},{10,8},{12,... | collective-permute-start | bytes 1769480 | tf_op jit(solution)/shard_map/ppermute | solution.py:14
  18.0 27.2 %collective-permute-start.1 = (bf16[15,1536]{0,1:T(8,128)(2,1)}, bf16[15,1536]{0,1:T(8,128)(2,1)S(1)}, u32[]{:S(2)}, u32[]{:S(2)}) collective-permute-start(bf16[15,1536]{0,1:T(8,128)(2,1)} %get-tuple-element.278), channel_id=1, source_target_pairs={{0,1},{2,3},{4,5},{6,7},{8,9},{10,11},{12,13},{14,15},{16,17},{18,... | collective-permute-start | bytes 138248 | tf_op jit(solution)/shard_map/ppermute | solution.py:22
  21.7 23.6 %collective-permute-start.2 = (bf16[15,1536]{0,1:T(8,128)(2,1)}, bf16[15,1536]{0,1:T(8,128)(2,1)S(1)}, u32[]{:S(2)}, u32[]{:S(2)}) collective-permute-start(bf16[15,1536]{0,1:T(8,128)(2,1)} %get-tuple-element.279), channel_id=1, source_target_pairs={{1,0},{3,2},{5,4},{7,6},{9,8},{11,10},{13,12},{15,14},{17,16},{19,... | collective-permute-start | bytes 138248 | tf_op jit(solution)/shard_map/ppermute | solution.py:25
  23.9 14.3 %all-to-all-start.1 = ((bf16[2,128,768]{1,2,0:T(8,128)(2,1)}), bf16[2,128,768]{1,2,0:T(8,128)(2,1)S(1)}, u32[]{:S(2)}, u32[]{:S(2)}) async-start(bf16[2,128,768]{1,2,0:T(8,128)(2,1)} %maximum_bitcast_fusion.1), calls=%async_computation.1 | async-start | bytes 786432 | tf_op jit(solution)/shard_map/all_to_all | solution.py:154
  28.0 17.3 %copy-start.45 = (f32[1536]{0:T(1024)}, f32[1536]{0:T(1024)S(1)}, u32[]{:S(2)}) copy-start(f32[1536]{0:T(1024)S(1)} %get-tuple-element.231) | copy-start | bytes 18436
  28.0 17.3 %copy-start.47 = (f32[1536]{0:T(1024)}, f32[1536]{0:T(1024)S(1)}, u32[]{:S(2)}) copy-start(f32[1536]{0:T(1024)S(1)} %get-tuple-element.232) | copy-start | bytes 18436
  28.0 17.3 %copy-start.49 = (f32[1536]{0:T(1024)}, f32[1536]{0:T(1024)S(1)}, u32[]{:S(2)}) copy-start(f32[1536]{0:T(1024)S(1)} %get-tuple-element.233) | copy-start | bytes 18436
  28.0 17.3 %copy-start.51 = (f32[1536]{0:T(1024)}, f32[1536]{0:T(1024)S(1)}, u32[]{:S(2)}) copy-start(f32[1536]{0:T(1024)S(1)} %get-tuple-element.234) | copy-start | bytes 18436
  28.0 17.3 %copy-start.53 = (f32[1536]{0:T(1024)}, f32[1536]{0:T(1024)S(1)}, u32[]{:S(2)}) copy-start(f32[1536]{0:T(1024)S(1)} %get-tuple-element.235) | copy-start | bytes 18436
  28.0 17.3 %copy-start.55 = (f32[1536]{0:T(1024)}, f32[1536]{0:T(1024)S(1)}, u32[]{:S(2)}) copy-start(f32[1536]{0:T(1024)S(1)} %get-tuple-element.236) | copy-start | bytes 18436
  28.0 17.3 %copy-start.57 = (f32[1536]{0:T(1024)}, f32[1536]{0:T(1024)S(1)}, u32[]{:S(2)}) copy-start(f32[1536]{0:T(1024)S(1)} %get-tuple-element.237) | copy-start | bytes 18436
  28.0 17.3 %copy-start.59 = (f32[1536]{0:T(1024)}, f32[1536]{0:T(1024)S(1)}, u32[]{:S(2)}) copy-start(f32[1536]{0:T(1024)S(1)} %get-tuple-element.238) | copy-start | bytes 18436
  28.1 17.3 %copy-start.61 = (f32[1536]{0:T(1024)}, f32[1536]{0:T(1024)S(1)}, u32[]{:S(2)}) copy-start(f32[1536]{0:T(1024)S(1)} %get-tuple-element.239) | copy-start | bytes 18436
  28.1 17.3 %copy-start.63 = (f32[1536]{0:T(1024)}, f32[1536]{0:T(1024)S(1)}, u32[]{:S(2)}) copy-start(f32[1536]{0:T(1024)S(1)} %get-tuple-element.240) | copy-start | bytes 18436
  28.1 17.3 %copy-start.65 = (f32[1536]{0:T(1024)}, f32[1536]{0:T(1024)S(1)}, u32[]{:S(2)}) copy-start(f32[1536]{0:T(1024)S(1)} %get-tuple-element.241) | copy-start | bytes 18436
  28.1 17.3 %copy-start.67 = (f32[1536]{0:T(1024)}, f32[1536]{0:T(1024)S(1)}, u32[]{:S(2)}) copy-start(f32[1536]{0:T(1024)S(1)} %get-tuple-element.242) | copy-start | bytes 18436
  28.4 17.0 %copy-start.11 = (f32[1536]{0:T(1024)}, f32[1536]{0:T(1024)S(1)}, u32[]{:S(2)}) copy-start(f32[1536]{0:T(1024)S(1)} %get-tuple-element.214) | copy-start | bytes 18436
  28.4 17.0 %copy-start.13 = (f32[1536]{0:T(1024)}, f32[1536]{0:T(1024)S(1)}, u32[]{:S(2)}) copy-start(f32[1536]{0:T(1024)S(1)} %get-tuple-element.215) | copy-start | bytes 18436
  28.4 17.0 %copy-start.15 = (f32[1536]{0:T(1024)}, f32[1536]{0:T(1024)S(1)}, u32[]{:S(2)}) copy-start(f32[1536]{0:T(1024)S(1)} %get-tuple-element.216) | copy-start | bytes 18436
  28.4 17.0 %copy-start.17 = (f32[1536]{0:T(1024)}, f32[1536]{0:T(1024)S(1)}, u32[]{:S(2)}) copy-start(f32[1536]{0:T(1024)S(1)} %get-tuple-element.217) | copy-start | bytes 18436
  28.4 17.0 %copy-start.19 = (f32[1536]{0:T(1024)}, f32[1536]{0:T(1024)S(1)}, u32[]{:S(2)}) copy-start(f32[1536]{0:T(1024)S(1)} %get-tuple-element.218) | copy-start | bytes 18436
  28.5 17.0 %copy-start.21 = (f32[1536]{0:T(1024)}, f32[1536]{0:T(1024)S(1)}, u32[]{:S(2)}) copy-start(f32[1536]{0:T(1024)S(1)} %get-tuple-element.219) | copy-start | bytes 18436
  28.5 17.0 %copy-start.23 = (f32[1536]{0:T(1024)}, f32[1536]{0:T(1024)S(1)}, u32[]{:S(2)}) copy-start(f32[1536]{0:T(1024)S(1)} %get-tuple-element.220) | copy-start | bytes 18436
  41.1 87.9 %all-to-all-start.2 = ((bf16[2,128,384]{2,1,0:T(8,128)(2,1)}), bf16[2,128,384]{2,1,0:T(8,128)(2,1)}, u32[]{:S(2)}, u32[]{:S(2)}) async-start(bf16[2,128,384]{2,1,0:T(8,128)(2,1)} %copy.86), calls=%async_computation.2 | async-start | bytes 393216 | tf_op jit(solution)/shard_map/all_to_all | solution.py:153
  45.2 130.0 %all-reduce.3.cloned.1.call-start = ((), (), s32[]{:S(2)}) async-start(), calls=%async_computation.5 | async-start | bytes 393216 | tf_op jit(solution)/shard_map/psum | solution.py:206
  45.3 19.1 %copy-start.1 = (bf16[15,1536]{0,1:T(8,128)(2,1)}, bf16[15,1536]{0,1:T(8,128)(2,1)S(1)}, u32[]{:S(2)}) copy-start(bf16[15,1536]{0,1:T(8,128)(2,1)S(1)} %collective-permute-done.2) | copy-start | bytes 138244
  108.9 19.8 %collective-permute-start.4 = (f32[15,1536]{1,0:T(8,128)}, f32[15,1536]{1,0:T(8,128)S(1)}, u32[]{:S(2)}, u32[]{:S(2)}) collective-permute-start(f32[15,1536]{1,0:T(8,128)} %copy.98), channel_id=1, source_target_pairs={{0,1},{2,3},{4,5},{6,7},{8,9},{10,11},{12,13},{14,15},{16,17},{18,... | collective-permute-start | bytes 276488 | tf_op jit(solution)/shard_map/ppermute | solution.py:22
  112.7 15.6 %collective-permute-start.3 = (f32[15,1536]{1,0:T(8,128)S(1)}, f32[15,1536]{1,0:T(8,128)S(1)}, u32[]{:S(2)}, u32[]{:S(2)}) collective-permute-start(f32[15,1536]{1,0:T(8,128)S(1)} %copy-done.10), channel_id=1, source_target_pairs={{1,0},{3,2},{5,4},{7,6},{9,8},{11,10},{13,12},{15,14},{17,16},{19,... | collective-permute-start | bytes 276488 | tf_op jit(solution)/shard_map/ppermute | solution.py:25
  148.7 28.3 %all-to-all-start.3 = ((bf16[2,128,768]{2,1,0:T(8,128)(2,1)}), bf16[2,128,768]{2,1,0:T(8,128)(2,1)S(1)}, u32[]{:S(2)}, u32[]{:S(2)}) async-start(bf16[2,128,768]{2,1,0:T(8,128)(2,1)} %copy.91), calls=%async_computation.3 | async-start | bytes 786432 | tf_op jit(solution)/shard_map/all_to_all | solution.py:165
  152.6 58.2 %all-reduce.5.cloned.1.call-start = ((), (), s32[]{:S(2)}) async-start(), calls=%async_computation.6 | async-start | bytes 380928 | tf_op jit(solution)/shard_map/psum | solution.py:206
  177.0 9.6 %all-to-all-start.4 = ((bf16[2,128,768]{2,1,0:T(8,128)(2,1)}), bf16[2,128,768]{2,1,0:T(8,128)(2,1)S(1)}, u32[]{:S(2)}, u32[]{:S(2)}) async-start(bf16[2,128,768]{2,1,0:T(8,128)(2,1)} %copy.94), calls=%async_computation.4 | async-start | bytes 786432 | tf_op jit(solution)/shard_map/all_to_all | solution.py:166
  (53 other events, 377.1 us)
Sparse Core Ops, SparseCore 0:
  107.2 25.4 all-reduce.2
  177.1 33.6 all-reduce.4
